TPU v7x, 128 devices: a whole 4x4x4 slice. The times are simulated.
128 devices in a mesh: ctx: 16 (over y, z_hi, core), tp: 8 (over z_lo, x).
Axes of the slice: x: 4, y: 4, z: 4 (z_hi: 2, z_lo: 2; z = z_hi * 2 + z_lo), core: 2. Of those that a mesh axis runs over, the one named last changes fastest.
Arguments:
- prompt_states: bfloat16 [2048, 1024], P('ctx'), may hold values from -1.5 to 1.5
- segment_ids: int32 [2048], P('ctx'), may hold values from 0 to 3, never falling along the last dimension, each value on 1 to 1024 neighbouring positions
- past_keys: bfloat16 [2048, 1024], P('ctx', 'tp'), may hold values from -1024 to 1024
- past_values: bfloat16 [2048, 1024], P('ctx', 'tp'), may hold values from -6 to 6
- cache_request: int32 [2048], P('ctx'), may hold values from 0 to 2, as said below
- decode_ids: int32 [4], replicated, may hold values from 0 to 32127
- embed_table: bfloat16 [32128, 1024], P(('ctx', 'tp')), may hold values from -6 to 6
- attn_gain: bfloat16 [1024], replicated, may hold values from 0.25 to 1.75
- ff_gain: bfloat16 [1024], replicated, may hold values from 0.25 to 1.75
- final_gain: bfloat16 [1024], replicated, may hold values from 0.25 to 1.75
- w_query: bfloat16 [1024, 1024], P(None, 'tp'), may hold values from -0.1875 to 0.1875
- w_key: bfloat16 [1024, 1024], P(None, 'tp'), may hold values from -0.1875 to 0.1875
- w_value: bfloat16 [1024, 1024], P(None, 'tp'), may hold values from -0.1875 to 0.1875
- w_out: bfloat16 [1024, 1024], P('tp'), may hold values from -0.1875 to 0.1875
- w_gate: bfloat16 [1024, 2816], P(None, 'tp'), may hold values from -0.1875 to 0.1875
- w_up: bfloat16 [1024, 2816], P(None, 'tp'), may hold values from -0.1875 to 0.1875
- w_down: bfloat16 [2816, 1024], P('tp'), may hold values from -0.109375 to 0.109375
- lm_head: bfloat16 [1024, 32128], P(None, ('ctx', 'tp')), may hold values from -0.1875 to 0.1875
Outputs:
- prompt_out: bfloat16 [2048, 1024], P('ctx')
- logits: float32 [4, 32128], P(None, ('ctx', 'tp'))
- relaid_keys: bfloat16 [2048, 1024], P(('ctx', 'tp'))
- relaid_values: bfloat16 [2048, 1024], P(('ctx', 'tp'))
Inputs may be any that keep to these rules, and one draw needn't show every extreme that they name: `cache_request`: only the even requests have cached rows, which may lie on any devices. `segment_ids`: the tokens of a request are consecutive; a request holds at most 1024 of them, and one request holds exactly that many.
All inputs are finite; a program needn't handle non-finite values.
Results may differ from a plain program's by a relative error of at most 0.03.
Values may be sent and summed in bfloat16 or wider, within the bound.
A program may use at most 64 MiB of HBM per device.

v0:
```python
import jax
import jax.numpy as jnp
from jax import lax
from jax.sharding import PartitionSpec as P

DH = 64
epsilon = 1e-06
scale_factor = 0.125
negative = -1e30


def joined(part, axis, combine):
    gathered = jax.tree.map(lambda a: lax.all_gather(a, axis), part)

    def take(source):
        return jax.tree.map(lambda a: lax.dynamic_index_in_dim(a, source, 0, False), gathered)

    return lax.fori_loop(
        1, lax.axis_size(axis), lambda source, state: combine(state, take(source)), take(0)
    )


def rms_norm(states, gain):
    states = states.astype(jnp.float32)
    mean_square = jnp.mean(states * states, axis=-1, keepdims=True)
    return (states * lax.rsqrt(mean_square + epsilon) * gain.astype(jnp.float32)).astype(
        jnp.bfloat16
    )


def partial_attend(queries, keys, values, allowed):
    scores = (
        jnp.einsum("qhd,khd->qhk", queries, keys, preferred_element_type=jnp.float32) * scale_factor
    )
    scores = jnp.where(allowed[:, None, :], scores, negative)
    highest = jnp.max(scores, axis=2)
    weights = jnp.where(allowed[:, None, :], jnp.exp(scores - highest[:, :, None]), 0.0)
    weight_sum = jnp.sum(weights, axis=2)
    summed = jnp.einsum(
        "qhk,khd->qhd", weights.astype(jnp.bfloat16), values, preferred_element_type=jnp.float32
    )
    return (highest, weight_sum, summed)


def join_parts(earlier, latter):
    highest = jnp.maximum(earlier[0], latter[0])
    left_scale = jnp.exp(earlier[0] - highest)
    right_scale = jnp.exp(latter[0] - highest)
    weight_sum = earlier[1] * left_scale + latter[1] * right_scale
    summed = earlier[2] * left_scale[:, :, None] + latter[2] * right_scale[:, :, None]
    return (highest, weight_sum, summed)


def finish(partials):
    return (partials[2] / partials[1][:, :, None]).astype(jnp.bfloat16)


def fold_block(running, query_heads, block_keys, block_values, allowed):
    key_count = block_keys.shape[0]
    head_group = query_heads.shape[1]

    def attend(current):
        return join_parts(
            current,
            partial_attend(
                query_heads,
                block_keys.reshape(key_count, head_group, DH),
                block_values.reshape(key_count, head_group, DH),
                allowed,
            ),
        )

    def unchanged(current):
        return current

    return lax.cond(jnp.any(allowed), attend, unchanged, running)


def gated_units(normed, w_gate, w_up, w_down):
    gate_value = jnp.dot(normed, w_gate, preferred_element_type=jnp.float32)
    up_value = jnp.dot(normed, w_up, preferred_element_type=jnp.float32)
    hidden = (jax.nn.gelu(gate_value, approximate=True) * up_value).astype(jnp.bfloat16)
    return jnp.dot(hidden, w_down, preferred_element_type=jnp.float32)


def project(normed, weight):
    return jnp.dot(normed, weight, preferred_element_type=jnp.float32).astype(jnp.bfloat16)


def on_device(
    prompt_states,
    segment_ids,
    past_keys,
    past_values,
    cache_request,
    decode_ids,
    embed_table,
    attn_gain,
    ff_gain,
    final_gain,
    w_query,
    w_key,
    w_value,
    w_out,
    w_gate,
    w_up,
    w_down,
    lm_head,
):
    row_count = prompt_states.shape[0]
    head_group = w_query.shape[1] // DH
    ctx_index = lax.axis_index("ctx")
    normed = rms_norm(prompt_states, attn_gain)
    queries = project(normed, w_query)
    keys = project(normed, w_key)
    values = project(normed, w_value)
    query_heads = queries.reshape(row_count, head_group, DH)
    q_positions = ctx_index * row_count + jnp.arange(row_count, dtype=jnp.int32)
    start_parts = (
        jnp.full((row_count, head_group), negative, jnp.float32),
        jnp.zeros((row_count, head_group), jnp.float32),
        jnp.zeros((row_count, head_group, DH), jnp.float32),
    )
    block_keys = lax.all_gather(keys, "ctx", axis=0, tiled=True)
    block_values = lax.all_gather(values, "ctx", axis=0, tiled=True)
    block_segment = lax.all_gather(segment_ids, "ctx", axis=0, tiled=True)
    key_positions = jnp.arange(block_segment.shape[0], dtype=jnp.int32)
    partials = fold_block(
        start_parts,
        query_heads,
        block_keys,
        block_values,
        (segment_ids[:, None] == block_segment[None, :])
        & (key_positions[None, :] <= q_positions[:, None]),
    )
    block_keys = lax.all_gather(past_keys, "ctx", axis=0, tiled=True)
    block_values = lax.all_gather(past_values, "ctx", axis=0, tiled=True)
    block_segment = lax.all_gather(cache_request, "ctx", axis=0, tiled=True)
    partials = fold_block(
        partials,
        query_heads,
        block_keys,
        block_values,
        segment_ids[:, None] == block_segment[None, :],
    )
    attended = finish(partials).reshape(row_count, head_group * DH)
    head_term = jnp.dot(attended, w_out, preferred_element_type=jnp.float32)
    residual = prompt_states.astype(jnp.float32) + lax.psum(
        head_term.astype(jnp.bfloat16), "tp"
    ).astype(jnp.float32)
    unit_term = gated_units(rms_norm(residual, ff_gain), w_gate, w_up, w_down)
    prompt_out = (
        residual + lax.psum(unit_term.astype(jnp.bfloat16), "tp").astype(jnp.float32)
    ).astype(jnp.bfloat16)
    relaid_keys, relaid_values = (
        lax.all_to_all(keys, "tp", split_axis=0, concat_axis=1, tiled=True),
        lax.all_to_all(values, "tp", split_axis=0, concat_axis=1, tiled=True),
    )
    vocab_rows = embed_table.shape[0]
    vocab_start = lax.axis_index(("ctx", "tp")) * vocab_rows
    one_hot = (
        decode_ids[:, None] == vocab_start + jnp.arange(vocab_rows, dtype=jnp.int32)[None, :]
    ).astype(jnp.bfloat16)
    embedded = lax.psum(
        jnp.dot(one_hot, embed_table, preferred_element_type=jnp.float32), ("ctx", "tp")
    )
    request_count = decode_ids.shape[0]
    decode_normed = rms_norm(embedded, attn_gain)
    decode_queries = project(decode_normed, w_query)
    decode_heads = decode_queries.reshape(request_count, head_group, DH)
    decode_keys = project(decode_normed, w_key).reshape(request_count, head_group, DH)
    decode_values = project(decode_normed, w_value).reshape(request_count, head_group, DH)
    requests = jnp.arange(request_count, dtype=jnp.int32)
    cache_count = past_keys.shape[0]
    cache_part = partial_attend(
        decode_heads,
        past_keys.reshape(cache_count, head_group, DH),
        past_values.reshape(cache_count, head_group, DH),
        requests[:, None] == cache_request[None, :],
    )
    prompt_part = partial_attend(
        decode_heads,
        keys.reshape(row_count, head_group, DH),
        values.reshape(row_count, head_group, DH),
        requests[:, None] == segment_ids[None, :],
    )
    gathered = joined(join_parts(prompt_part, cache_part), "ctx", join_parts)
    own_part = partial_attend(
        decode_heads, decode_keys, decode_values, requests[:, None] == requests[None, :]
    )
    decode_attended = finish(join_parts(gathered, own_part)).reshape(request_count, head_group * DH)
    decode_residual = embedded + lax.psum(
        jnp.dot(decode_attended, w_out, preferred_element_type=jnp.float32), "tp"
    )
    decode_term = gated_units(rms_norm(decode_residual, ff_gain), w_gate, w_up, w_down)
    decode_final = decode_residual + lax.psum(decode_term, "tp")
    logits = jnp.dot(
        rms_norm(decode_final, final_gain), lm_head, preferred_element_type=jnp.float32
    )
    return (prompt_out, logits, relaid_keys, relaid_values)


def solution(mesh):
    placed = (
        P("ctx", None),
        P("ctx"),
        P("ctx", "tp"),
        P("ctx", "tp"),
        P("ctx"),
        P(),
        P(("ctx", "tp"), None),
        P(),
        P(),
        P(),
        P(None, "tp"),
        P(None, "tp"),
        P(None, "tp"),
        P("tp", None),
        P(None, "tp"),
        P(None, "tp"),
        P("tp", None),
        P(None, ("ctx", "tp")),
    )
    return jax.shard_map(
        on_device,
        mesh=mesh,
        in_specs=placed,
        out_specs=(
            P("ctx", None),
            P(None, ("ctx", "tp")),
            P(("ctx", "tp"), None),
            P(("ctx", "tp"), None),
        ),
        check_vma=False,
    )
```

profile of v0, /device:TPU:0, one launch (start us, length us, event | category | flops | bytes accessed | tf_op | source)
XLA Modules:
  0.0 462.5 jit_solution(8723615287294162902)
XLA Ops:
  7.3 25.5 %all-gather.2 = s32[16,1,128]{2,1,0:T(1,128)S(1)} all-gather(s32[1,1,128]{2,1,0:T(1,128)} %bitcast.173), channel_id=1, replica_groups=mesh['ctx'=16,'tp'=8] {'ctx'}, dimensions={0}, use_global_device_ids=true | all-gather | bytes 8704 | tf_op jit(solution)/shard_map/all_gather | solution.py:126
  32.8 19.3 %all-gather.1 = s32[16,1,128]{2,1,0:T(1,128)S(1)} all-gather(s32[1,1,128]{2,1,0:T(1,128)} %bitcast.174), channel_id=1, replica_groups=mesh['ctx'=16,'tp'=8] {'ctx'}, dimensions={0}, use_global_device_ids=true | all-gather | bytes 8704 | tf_op jit(solution)/shard_map/all_gather | solution.py:138
  52.1 3.4 fusion.125
  56.8 0.7 convert_element_type.100
  57.4 1.1 fusion.44
  58.5 1.9 convolution_convert_fusion.4
  60.5 23.8 %all_gather.34 = bf16[2048,128]{1,0:T(8,128)(2,1)S(1)} all-gather(bf16[128,128]{1,0:T(8,128)(2,1)} %convolution_convert_fusion.4), channel_id=1, replica_groups=mesh['ctx'=16,'tp'=8] {'ctx'}, dimensions={0}, use_global_device_ids=true | all-gather | bytes 557056 | tf_op jit(solution)/shard_map/all_gather | solution.py:124
  84.6 0.9 convolution_convert_fusion.2
  85.5 22.3 %all_gather.35 = bf16[2048,128]{1,0:T(8,128)(2,1)} all-gather(bf16[128,128]{1,0:T(8,128)(2,1)} %convolution_convert_fusion.2), channel_id=1, replica_groups=mesh['ctx'=16,'tp'=8] {'ctx'}, dimensions={0}, use_global_device_ids=true | all-gather | bytes 557056 | tf_op jit(solution)/shard_map/all_gather | solution.py:125
  108.0 25.2 %all_gather.36 = bf16[2048,128]{0,1:T(8,128)(2,1)} all-gather(bf16[128,128]{0,1:T(8,128)(2,1)S(1)} %copy.75), channel_id=1, replica_groups=mesh['ctx'=16,'tp'=8] {'ctx'}, dimensions={0}, use_global_device_ids=true | all-gather | bytes 557056 | tf_op jit(solution)/shard_map/all_gather | solution.py:136
  133.3 22.1 %all_gather.37 = bf16[2048,128]{0,1:T(8,128)(2,1)} all-gather(bf16[128,128]{0,1:T(8,128)(2,1)S(1)} %copy.76), channel_id=1, replica_groups=mesh['ctx'=16,'tp'=8] {'ctx'}, dimensions={0}, use_global_device_ids=true | all-gather | bytes 557056 | tf_op jit(solution)/shard_map/all_gather | solution.py:137
  155.4 8.3 %conditional.2 = (f32[128,2]{0,1:T(2,128)}, f32[128,2]{0,1:T(2,128)S(1)}, f32[128,2,64]{0,2,1:T(8,128)S(1)}) conditional(s32[]{:T(128)} %convert_element_type.99, () %tuple.45, (pred[128,2048]{0,1:T(8,128)(4,1)}, bf16[2048,128]{1,0:T(8,128)(2,1)S(1)}, bf16[128,2,64]{0,2,1:T(8,128)(2,1)S(1)}, bf16[2048,128]{1,0:T(8,128)(2,1)}) %tuple.100), branch_computations={%region_3.4_spmd, %region_4.7_spmd} | conditional | flops 138970624 | bytes 11384884 | solution.py:76
  155.4 1.0 copy.73
  156.5 1.8 fusion.131
  158.2 0.6 exponential_multiply_fusion
  159.2 0.7 multiply_add_fusion
  159.9 2.1 copy.74
  162.0 1.7 fusion.5
  163.8 3.6 conditional.3
  163.8 1.8 fusion.132
  165.6 0.4 fusion.14
  166.0 0.7 multiply_add_fusion.1
  166.7 0.7 fusion.16
  167.4 1.0 convolution_convert_fusion.1
  168.4 4.9 %all-to-all-start = ((bf16[8,16,128]{2,1,0:T(8,128)(2,1)}), bf16[8,16,128]{2,1,0:T(8,128)(2,1)S(1)}, u32[]{:S(2)}, u32[]{:S(2)}) async-start(bf16[8,16,128]{2,1,0:T(8,128)(2,1)} %bitcast.34), calls=%async_computation | async-start | bytes 65536 | tf_op jit(solution)/shard_map/all_to_all | solution.py:156
  173.4 0.9 copy.77
  174.3 0.9 copy.81
  175.4 66.9 %psum.37 = f32[4,1024]{1,0:T(4,128)S(1)} all-reduce(f32[4,1024]{1,0:T(4,128)S(1)} %fusion.70), channel_id=1, replica_groups=mesh['ctx'=16,'tp'=8] {'ctx','tp'}, use_global_device_ids=true, to_apply=%region_14.15 | all-reduce | flops 4096 | bytes 32768 | tf_op jit(solution)/shard_map/psum | solution.py:164
  242.5 1.1 convolution_convert_fusion.7
  243.6 1.1 convolution_convert_fusion.6
  244.8 1.2 convolution_convert_fusion.5
  246.8 22.7 %all_gather.38 = f32[16,4,2]{1,2,0:T(2,128)S(1)} all-gather(f32[1,4,2]{1,2,0:T(2,128)S(1)} %get-tuple-element.301), channel_id=1, replica_groups=mesh['ctx'=16,'tp'=8] {'ctx'}, dimensions={0}, use_global_device_ids=true | all-gather | bytes 544 | tf_op jit(solution)/shard_map/all_gather | solution.py:13
  269.5 19.2 %all_gather.39 = f32[16,4,2]{1,2,0:T(2,128)S(1)} all-gather(f32[1,4,2]{1,2,0:T(2,128)S(1)} %get-tuple-element.300), channel_id=1, replica_groups=mesh['ctx'=16,'tp'=8] {'ctx'}, dimensions={0}, use_global_device_ids=true | all-gather | bytes 544 | tf_op jit(solution)/shard_map/all_gather | solution.py:13
  289.1 22.3 %all-gather = f32[64,2,64]{2,1,0:T(2,128)S(1)} all-gather(f32[4,2,64]{2,1,0:T(2,128)S(1)} %copy.83), channel_id=2, replica_groups=mesh['ctx'=16,'tp'=8] {'ctx'}, dimensions={0}, use_global_device_ids=true | all-gather | bytes 34816 | tf_op jit(solution)/shard_map/all_gather | solution.py:13
  311.4 4.4 while.19
  316.6 31.3 %psum.38 = f32[4,1024]{1,0:T(4,128)S(1)} all-reduce(f32[4,1024]{1,0:T(4,128)S(1)} %fusion.136), channel_id=1, replica_groups=mesh['ctx'=16,'tp'=8] {'tp'}, use_global_device_ids=true, to_apply=%region_24.25 | all-reduce | flops 4096 | bytes 32768 | tf_op jit(solution)/shard_map/psum | solution.py:192
  348.4 0.7 fusion.42
  349.0 30.6 %psum.39 = f32[4,1024]{1,0:T(4,128)S(1)} all-reduce(f32[4,1024]{1,0:T(4,128)S(1)} %fusion.42), channel_id=1, replica_groups=mesh['ctx'=16,'tp'=8] {'tp'}, use_global_device_ids=true, to_apply=%region_26.27 | all-reduce | flops 4096 | bytes 32768 | tf_op jit(solution)/shard_map/psum | solution.py:196
  379.8 0.8 fusion.59
  380.6 1.2 multiply_reduce_fusion
  381.8 1.4 fusion.120
  383.2 1.7 convolution_convert_fusion
  384.9 3.3 all-to-all-start.1
  388.3 0.6 copy_bitcast_fusion.1
  388.9 5.6 %all-to-all-done.1 = bf16[8,16,128]{2,1,0:T(8,128)(2,1)S(1)} async-done(((bf16[8,16,128]{2,1,0:T(8,128)(2,1)}), bf16[8,16,128]{2,1,0:T(8,128)(2,1)S(1)}, u32[]{:S(2)}, u32[]{:S(2)}) %all-to-all-start.1) | async-done | bytes 32800 | tf_op jit(solution)/shard_map/all_to_all | solution.py:157
  394.5 0.6 copy_bitcast_fusion
  395.1 58.8 %all-reduce.5.cloned.1.call-done = bf16[128,1024]{1,0:T(8,128)(2,1)} async-done(((bf16[128,1024]{1,0:T(8,128)(2,1)}), bf16[128,1024]{1,0:T(8,128)(2,1)}) %all-reduce.5.cloned.1.call-update) | async-done | bytes 262160 | tf_op jit(solution)/shard_map/psum | solution.py:153
  453.9 1.8 add_convert_fusion
  (149 shorter events, 8.6 us)
Async XLA Ops:
  7.2 341.2 %copy-start = (bf16[352,1024]{1,0:T(8,128)(2,1)S(1)}, bf16[352,1024]{1,0:T(8,128)(2,1)}, u32[]{:S(2)}) copy-start(bf16[352,1024]{1,0:T(8,128)(2,1)} %param.40) | copy-start | bytes 2162692
  7.2 77.1 %copy-start.1 = (bf16[128,1024]{1,0:T(8,128)(2,1)S(1)}, bf16[128,1024]{1,0:T(8,128)(2,1)}, u32[]{:S(2)}) copy-start(bf16[128,1024]{1,0:T(8,128)(2,1)} %param.24) | copy-start | bytes 786436
  7.2 77.1 %copy-start.10 = (bf16[1024,128]{1,0:T(8,128)(2,1)S(1)}, bf16[1024,128]{1,0:T(8,128)(2,1)}, u32[]{:S(2)}) copy-start(bf16[1024,128]{1,0:T(8,128)(2,1)} %param.34) | copy-start | bytes 786436
  7.2 77.4 %copy-start.11 = (bf16[1024,128]{1,0:T(8,128)(2,1)S(1)}, bf16[1024,128]{1,0:T(8,128)(2,1)}, u32[]{:S(2)}) copy-start(bf16[1024,128]{1,0:T(8,128)(2,1)} %param.36) | copy-start | bytes 786436
  7.2 100.6 %copy-start.12 = (bf16[128,128]{1,0:T(8,128)(2,1)S(1)}, bf16[128,128]{1,0:T(8,128)(2,1)}, u32[]{:S(2)}) copy-start(bf16[128,128]{1,0:T(8,128)(2,1)} %param.26) | copy-start | bytes 98308
  7.2 373.4 %all-reduce.3.cloned.1.call-start = ((), (), s32[]{:S(2)}) async-start(), calls=%async_computation.2 | async-start | bytes 524288 | tf_op jit(solution)/shard_map/psum | solution.py:148
  55.5 77.7 %copy-start.13 = (bf16[128,128]{1,0:T(8,128)(2,1)S(1)}, bf16[128,128]{1,0:T(8,128)(2,1)}, u32[]{:S(2)}) copy-start(bf16[128,128]{1,0:T(8,128)(2,1)} %param.27) | copy-start | bytes 98308
  156.4 2.4 copy-start.5
  163.7 3.7 copy-start.6
  163.7 9.7 %copy-start.18 = (s32[128]{0:T(128)S(1)}, s32[128]{0:T(128)}, u32[]{:S(2)}) copy-start(s32[128]{0:T(128)} %param.28) | copy-start | bytes 1540
  163.7 10.5 %copy-start.16 = (s32[128]{0:T(128)S(1)}, s32[128]{0:T(128)}, u32[]{:S(2)}) copy-start(s32[128]{0:T(128)} %param.25) | copy-start | bytes 1540
  163.7 11.4 %copy-start.7 = (bf16[251,1024]{1,0:T(8,128)(2,1)S(1)}, bf16[251,1024]{1,0:T(8,128)(2,1)}, u32[]{:S(2)}) copy-start(bf16[251,1024]{1,0:T(8,128)(2,1)} %param.30) | copy-start | bytes 1542148
  163.7 11.4 %copy-start.17 = (s32[4]{0:T(128)S(1)}, s32[4]{0:T(128)}, u32[]{:S(2)}) copy-start(s32[4]{0:T(128)} %param.29) | copy-start | bytes 52
  163.8 2.9 copy-start.9
  167.4 78.5 %copy-start.14 = (bf16[1024]{0:T(1024)(128)(2,1)S(1)}, bf16[1024]{0:T(1024)(128)(2,1)}, u32[]{:S(2)}) copy-start(bf16[1024]{0:T(1024)(128)(2,1)} %param.32) | copy-start | bytes 6148
  167.4 180.7 %copy-start.3 = (bf16[1024,352]{0,1:T(8,128)(2,1)S(1)}, bf16[1024,352]{0,1:T(8,128)(2,1)}, u32[]{:S(2)}) copy-start(bf16[1024,352]{0,1:T(8,128)(2,1)} %param.38) | copy-start | bytes 2162692
  168.4 180.0 %copy-start.4 = (bf16[1024,352]{0,1:T(8,128)(2,1)S(1)}, bf16[1024,352]{0,1:T(8,128)(2,1)}, u32[]{:S(2)}) copy-start(bf16[1024,352]{0,1:T(8,128)(2,1)} %param.39) | copy-start | bytes 2162692
  168.4 216.5 %all-to-all-start = ((bf16[8,16,128]{2,1,0:T(8,128)(2,1)}), bf16[8,16,128]{2,1,0:T(8,128)(2,1)S(1)}, u32[]{:S(2)}, u32[]{:S(2)}) async-start(bf16[8,16,128]{2,1,0:T(8,128)(2,1)} %bitcast.34), calls=%async_computation | async-start | bytes 65536 | tf_op jit(solution)/shard_map/all_to_all | solution.py:156
  173.3 280.5 %all-reduce.5.cloned.1.call-start = ((), (), s32[]{:S(2)}) async-start(), calls=%async_computation.3 | async-start | bytes 524288 | tf_op jit(solution)/shard_map/psum | solution.py:153
  244.7 135.1 %copy-start.15 = (bf16[1024]{0:T(1024)(128)(2,1)S(1)}, bf16[1024]{0:T(1024)(128)(2,1)}, u32[]{:S(2)}) copy-start(bf16[1024]{0:T(1024)(128)(2,1)} %param.33) | copy-start | bytes 6148
  244.7 135.1 %copy-start.8 = (bf16[1024,251]{1,0:T(8,128)(2,1)S(1)}, bf16[1024,251]{1,0:T(8,128)(2,1)}, u32[]{:S(2)}) copy-start(bf16[1024,251]{1,0:T(8,128)(2,1)} %param.41) | copy-start | bytes 1542148
  380.6 2.6 copy-start.2
  384.9 9.5 %all-to-all-start.1 = ((bf16[8,16,128]{2,1,0:T(8,128)(2,1)}), bf16[8,16,128]{2,1,0:T(8,128)(2,1)S(1)}, u32[]{:S(2)}, u32[]{:S(2)}) async-start(bf16[8,16,128]{2,1,0:T(8,128)(2,1)} %bitcast.36), calls=%async_computation.1 | async-start | bytes 65536 | tf_op jit(solution)/shard_map/all_to_all | solution.py:157
Sparse Core Ops, SparseCore 0:
  168.5 73.1 all-reduce.2
  385.0 68.7 all-reduce.4
where the time goes:
time: 464 us; the launch traced here: 462 us
  blocking collectives  331 us (71%)
  waiting for transfers between devices  64.4 us (14%)
  matrix products  19.7 us (4%)
  between operations  15.7 us (3%)
  other arithmetic  13.4 us (3%)
  local copies, waits for them, and re-layouts  9.55 us (2%)
  starting transfers between devices  8.32 us (2%)
    psum x1, blocking collectives, on_device(): lax.psum(jnp.dot(one_hot, embed_table, preferred_element_type=jnp.float32...  66.9 us
    all_gather x3, blocking collectives, joined(): gathered = jax.tree.map(lambda a: lax.all_gather(a, axis), part)  64.2 us
    psum x1, waiting for transfers between devices, on_device(): lax.psum(unit_term.astype(jnp.bfloat16), 'tp').astype(jnp.float32)  58.8 us
    psum x1, blocking collectives, on_device(): lax.psum(jnp.dot(decode_attended, w_out, preferred_element_type=jnp.float...  31.3 us
    psum x1, blocking collectives, on_device(): decode_final = decode_residual + lax.psum(decode_term, 'tp')  30.6 us
    all_gather x1, blocking collectives, on_device(): block_segment = lax.all_gather(segment_ids, 'ctx', axis=0, tiled=True)  25.5 us
    all_gather x1, blocking collectives, on_device(): block_keys = lax.all_gather(past_keys, 'ctx', axis=0, tiled=True)  25.2 us
    all_gather x1, blocking collectives, on_device(): block_keys = lax.all_gather(keys, 'ctx', axis=0, tiled=True)  23.8 us
  transfers between devices with their start and end apart: 4, of which 2 were waited for; matrix products, arithmetic and copies ran while one was open for 4% of the time, Pallas kernels for 0%

commit v1 on v0

--- a/solution.py
+++ b/solution.py
@@ -7,6 +7,12 @@
 epsilon = 1e-06
 scale_factor = 0.125
 negative = -1e30
+
+
+def add_all(x, axis):
+    parts = lax.all_gather(x, axis, axis=0, tiled=False)
+    summed = parts.sum(axis=0)
+    return summed
 
 
 def joined(part, axis, combine):
@@ -189,7 +195,7 @@
         decode_heads, decode_keys, decode_values, requests[:, None] == requests[None, :]
     )
     decode_attended = finish(join_parts(gathered, own_part)).reshape(request_count, head_group * DH)
-    decode_residual = embedded + lax.psum(
+    decode_residual = embedded + add_all(
         jnp.dot(decode_attended, w_out, preferred_element_type=jnp.float32), "tp"
     )
     decode_term = gated_units(rms_norm(decode_residual, ff_gain), w_gate, w_up, w_down)

time: 464 us -> 461 us (level)
    psum x1 -> x0, blocking collectives: 31.3 us -> none  [on_device(): lax.psum(jnp.dot(decode_attended, w_out, preferred_element_type=jnp.float...]
    all_gather x0 -> x1, blocking collectives: none -> 28.2 us  [add_all(): parts = lax.all_gather(x, axis, axis=0, tiled=False)]
where the time goes in v1:
time: 461 us; the launch traced here: 460 us
  blocking collectives  329 us (71%)
  waiting for transfers between devices  64.6 us (14%)
  matrix products  19.6 us (4%)
  between operations  15.7 us (3%)
  other arithmetic  13.4 us (3%)
  local copies, waits for them, and re-layouts  9.62 us (2%)
  starting transfers between devices  8.19 us (2%)
    psum x1, blocking collectives, on_device(): lax.psum(jnp.dot(one_hot, embed_table, preferred_element_type=jnp.float32...  67 us
    all_gather x3, blocking collectives, joined(): gathered = jax.tree.map(lambda a: lax.all_gather(a, axis), part)  64.1 us
    psum x1, waiting for transfers between devices, on_device(): lax.psum(unit_term.astype(jnp.bfloat16), 'tp').astype(jnp.float32)  58.9 us
    psum x1, blocking collectives, on_device(): decode_final = decode_residual + lax.psum(decode_term, 'tp')  31.4 us
    all_gather x1, blocking collectives, add_all(): parts = lax.all_gather(x, axis, axis=0, tiled=False)  28.2 us
    all_gather x1, blocking collectives, on_device(): block_segment = lax.all_gather(segment_ids, 'ctx', axis=0, tiled=True)  25.5 us
    all_gather x1, blocking collectives, on_device(): block_keys = lax.all_gather(past_keys, 'ctx', axis=0, tiled=True)  25.2 us
    all_gather x1, blocking collectives, on_device(): block_keys = lax.all_gather(keys, 'ctx', axis=0, tiled=True)  23.8 us
  transfers between devices with their start and end apart: 4, of which 2 were waited for; matrix products, arithmetic and copies ran while one was open for 4% of the time, Pallas kernels for 0%

profile of v1, /device:TPU:0, one launch (start us, length us, event | category | flops | bytes accessed | tf_op | source)
XLA Modules:
  0.0 460.1 jit_solution(3018082631574060940)
XLA Ops:
  7.3 25.5 %all-gather.3 = s32[16,1,128]{2,1,0:T(1,128)S(1)} all-gather(s32[1,1,128]{2,1,0:T(1,128)} %bitcast.175), channel_id=1, replica_groups=mesh['ctx'=16,'tp'=8] {'ctx'}, dimensions={0}, use_global_device_ids=true | all-gather | bytes 8704 | tf_op jit(solution)/shard_map/all_gather | solution.py:132
  32.8 19.3 %all-gather.2 = s32[16,1,128]{2,1,0:T(1,128)S(1)} all-gather(s32[1,1,128]{2,1,0:T(1,128)} %bitcast.176), channel_id=1, replica_groups=mesh['ctx'=16,'tp'=8] {'ctx'}, dimensions={0}, use_global_device_ids=true | all-gather | bytes 8704 | tf_op jit(solution)/shard_map/all_gather | solution.py:144
  52.1 3.4 fusion.125
  56.8 0.7 convert_element_type.100
  57.4 1.1 fusion.44
  58.5 1.9 convolution_convert_fusion.4
  60.5 23.8 %all_gather.40 = bf16[2048,128]{1,0:T(8,128)(2,1)S(1)} all-gather(bf16[128,128]{1,0:T(8,128)(2,1)} %convolution_convert_fusion.4), channel_id=1, replica_groups=mesh['ctx'=16,'tp'=8] {'ctx'}, dimensions={0}, use_global_device_ids=true | all-gather | bytes 557056 | tf_op jit(solution)/shard_map/all_gather | solution.py:130
  84.6 0.9 convolution_convert_fusion.2
  85.5 22.3 %all_gather.41 = bf16[2048,128]{1,0:T(8,128)(2,1)} all-gather(bf16[128,128]{1,0:T(8,128)(2,1)} %convolution_convert_fusion.2), channel_id=1, replica_groups=mesh['ctx'=16,'tp'=8] {'ctx'}, dimensions={0}, use_global_device_ids=true | all-gather | bytes 557056 | tf_op jit(solution)/shard_map/all_gather | solution.py:131
  108.0 25.2 %all_gather.42 = bf16[2048,128]{0,1:T(8,128)(2,1)} all-gather(bf16[128,128]{0,1:T(8,128)(2,1)S(1)} %copy.75), channel_id=1, replica_groups=mesh['ctx'=16,'tp'=8] {'ctx'}, dimensions={0}, use_global_device_ids=true | all-gather | bytes 557056 | tf_op jit(solution)/shard_map/all_gather | solution.py:142
  133.3 22.1 %all_gather.43 = bf16[2048,128]{0,1:T(8,128)(2,1)} all-gather(bf16[128,128]{0,1:T(8,128)(2,1)S(1)} %copy.76), channel_id=1, replica_groups=mesh['ctx'=16,'tp'=8] {'ctx'}, dimensions={0}, use_global_device_ids=true | all-gather | bytes 557056 | tf_op jit(solution)/shard_map/all_gather | solution.py:143
  155.4 8.3 %conditional.2 = (f32[128,2]{0,1:T(2,128)}, f32[128,2]{0,1:T(2,128)S(1)}, f32[128,2,64]{0,2,1:T(8,128)S(1)}) conditional(s32[]{:T(128)} %convert_element_type.99, () %tuple.45, (pred[128,2048]{0,1:T(8,128)(4,1)}, bf16[2048,128]{1,0:T(8,128)(2,1)S(1)}, bf16[128,2,64]{0,2,1:T(8,128)(2,1)S(1)}, bf16[2048,128]{1,0:T(8,128)(2,1)}) %tuple.100), branch_computations={%region_3.4_spmd, %region_4.7_spmd} | conditional | flops 138970624 | bytes 11384884 | solution.py:82
  155.4 1.0 copy.73
  156.5 1.8 fusion.131
  158.2 0.6 exponential_multiply_fusion
  159.2 0.7 multiply_add_fusion
  159.9 2.1 copy.74
  162.0 1.7 fusion.5
  163.8 3.6 conditional.3
  163.8 1.8 fusion.132
  165.6 0.4 fusion.14
  166.0 0.7 multiply_add_fusion.1
  166.7 0.7 fusion.16
  167.4 1.0 convolution_convert_fusion.1
  168.4 4.8 %all-to-all-start = ((bf16[8,16,128]{2,1,0:T(8,128)(2,1)}), bf16[8,16,128]{2,1,0:T(8,128)(2,1)S(1)}, u32[]{:S(2)}, u32[]{:S(2)}) async-start(bf16[8,16,128]{2,1,0:T(8,128)(2,1)} %bitcast.35), calls=%async_computation | async-start | bytes 65536 | tf_op jit(solution)/shard_map/all_to_all | solution.py:162
  173.3 0.9 copy.77
  174.2 0.9 copy.81
  175.3 67.0 %psum.30 = f32[4,1024]{1,0:T(4,128)S(1)} all-reduce(f32[4,1024]{1,0:T(4,128)S(1)} %fusion.70), channel_id=1, replica_groups=mesh['ctx'=16,'tp'=8] {'ctx','tp'}, use_global_device_ids=true, to_apply=%region_14.15 | all-reduce | flops 4096 | bytes 32768 | tf_op jit(solution)/shard_map/psum | solution.py:170
  242.5 1.1 convolution_convert_fusion.7
  243.6 1.1 convolution_convert_fusion.6
  244.7 1.1 convolution_convert_fusion.5
  246.7 22.5 %all_gather.44 = f32[16,4,2]{1,2,0:T(2,128)S(1)} all-gather(f32[1,4,2]{1,2,0:T(2,128)S(1)} %get-tuple-element.301), channel_id=1, replica_groups=mesh['ctx'=16,'tp'=8] {'ctx'}, dimensions={0}, use_global_device_ids=true | all-gather | bytes 544 | tf_op jit(solution)/shard_map/all_gather | solution.py:19
  269.3 19.2 %all_gather.45 = f32[16,4,2]{1,2,0:T(2,128)S(1)} all-gather(f32[1,4,2]{1,2,0:T(2,128)S(1)} %get-tuple-element.300), channel_id=1, replica_groups=mesh['ctx'=16,'tp'=8] {'ctx'}, dimensions={0}, use_global_device_ids=true | all-gather | bytes 544 | tf_op jit(solution)/shard_map/all_gather | solution.py:19
  288.9 22.3 %all-gather = f32[64,2,64]{2,1,0:T(2,128)S(1)} all-gather(f32[4,2,64]{2,1,0:T(2,128)S(1)} %copy.83), channel_id=2, replica_groups=mesh['ctx'=16,'tp'=8] {'ctx'}, dimensions={0}, use_global_device_ids=true | all-gather | bytes 34816 | tf_op jit(solution)/shard_map/all_gather | solution.py:19
  311.2 4.4 while.19
  316.4 28.2 %all-gather.4 = f32[8,4,1024]{2,1,0:T(4,128)S(1)} all-gather(f32[1,4,1024]{2,1,0:T(4,128)S(1)} %convolution_bitcast_fusion.2), channel_id=3, replica_groups=mesh['ctx'=16,'tp'=8] {'tp'}, dimensions={0}, use_global_device_ids=true | all-gather | bytes 147456 | tf_op jit(solution)/shard_map/all_gather | solution.py:13
  345.0 0.7 fusion.42
  345.7 31.4 %psum.31 = f32[4,1024]{1,0:T(4,128)S(1)} all-reduce(f32[4,1024]{1,0:T(4,128)S(1)} %fusion.42), channel_id=1, replica_groups=mesh['ctx'=16,'tp'=8] {'tp'}, use_global_device_ids=true, to_apply=%region_26.27 | all-reduce | flops 4096 | bytes 32768 | tf_op jit(solution)/shard_map/psum | solution.py:202
  377.2 0.8 fusion.59
  378.1 1.2 multiply_reduce_fusion
  379.3 1.4 fusion.120
  380.6 1.7 convolution_convert_fusion
  382.3 3.3 all-to-all-start.1
  385.7 0.6 copy_bitcast_fusion.1
  386.3 5.6 %all-to-all-done.1 = bf16[8,16,128]{2,1,0:T(8,128)(2,1)S(1)} async-done(((bf16[8,16,128]{2,1,0:T(8,128)(2,1)}), bf16[8,16,128]{2,1,0:T(8,128)(2,1)S(1)}, u32[]{:S(2)}, u32[]{:S(2)}) %all-to-all-start.1) | async-done | bytes 32800 | tf_op jit(solution)/shard_map/all_to_all | solution.py:163
  391.9 0.6 copy_bitcast_fusion
  392.5 58.9 %all-reduce.5.cloned.1.call-done = bf16[128,1024]{1,0:T(8,128)(2,1)} async-done(((bf16[128,1024]{1,0:T(8,128)(2,1)}), bf16[128,1024]{1,0:T(8,128)(2,1)}) %all-reduce.5.cloned.1.call-update) | async-done | bytes 262160 | tf_op jit(solution)/shard_map/psum | solution.py:159
  451.4 1.8 add_convert_fusion
  (150 shorter events, 8.6 us)
Async XLA Ops:
  7.2 337.9 %copy-start = (bf16[352,1024]{1,0:T(8,128)(2,1)S(1)}, bf16[352,1024]{1,0:T(8,128)(2,1)}, u32[]{:S(2)}) copy-start(bf16[352,1024]{1,0:T(8,128)(2,1)} %param.40) | copy-start | bytes 2162692
  7.2 77.1 %copy-start.1 = (bf16[128,1024]{1,0:T(8,128)(2,1)S(1)}, bf16[128,1024]{1,0:T(8,128)(2,1)}, u32[]{:S(2)}) copy-start(bf16[128,1024]{1,0:T(8,128)(2,1)} %param.24) | copy-start | bytes 786436
  7.2 77.1 %copy-start.10 = (bf16[1024,128]{1,0:T(8,128)(2,1)S(1)}, bf16[1024,128]{1,0:T(8,128)(2,1)}, u32[]{:S(2)}) copy-start(bf16[1024,128]{1,0:T(8,128)(2,1)} %param.34) | copy-start | bytes 786436
  7.2 77.4 %copy-start.11 = (bf16[1024,128]{1,0:T(8,128)(2,1)S(1)}, bf16[1024,128]{1,0:T(8,128)(2,1)}, u32[]{:S(2)}) copy-start(bf16[1024,128]{1,0:T(8,128)(2,1)} %param.36) | copy-start | bytes 786436
  7.2 100.6 %copy-start.12 = (bf16[128,128]{1,0:T(8,128)(2,1)S(1)}, bf16[128,128]{1,0:T(8,128)(2,1)}, u32[]{:S(2)}) copy-start(bf16[128,128]{1,0:T(8,128)(2,1)} %param.26) | copy-start | bytes 98308
  7.2 370.8 %all-reduce.3.cloned.1.call-start = ((), (), s32[]{:S(2)}) async-start(), calls=%async_computation.2 | async-start | bytes 524288 | tf_op jit(solution)/shard_map/psum | solution.py:154
  55.5 77.7 %copy-start.13 = (bf16[128,128]{1,0:T(8,128)(2,1)S(1)}, bf16[128,128]{1,0:T(8,128)(2,1)}, u32[]{:S(2)}) copy-start(bf16[128,128]{1,0:T(8,128)(2,1)} %param.27) | copy-start | bytes 98308
  156.4 2.4 copy-start.5
  163.7 3.7 copy-start.6
  163.7 9.5 %copy-start.18 = (s32[128]{0:T(128)S(1)}, s32[128]{0:T(128)}, u32[]{:S(2)}) copy-start(s32[128]{0:T(128)} %param.28) | copy-start | bytes 1540
  163.7 10.5 %copy-start.16 = (s32[128]{0:T(128)S(1)}, s32[128]{0:T(128)}, u32[]{:S(2)}) copy-start(s32[128]{0:T(128)} %param.25) | copy-start | bytes 1540
  163.7 11.4 %copy-start.7 = (bf16[251,1024]{1,0:T(8,128)(2,1)S(1)}, bf16[251,1024]{1,0:T(8,128)(2,1)}, u32[]{:S(2)}) copy-start(bf16[251,1024]{1,0:T(8,128)(2,1)} %param.30) | copy-start | bytes 1542148
  163.7 11.4 %copy-start.17 = (s32[4]{0:T(128)S(1)}, s32[4]{0:T(128)}, u32[]{:S(2)}) copy-start(s32[4]{0:T(128)} %param.29) | copy-start | bytes 52
  163.8 2.9 copy-start.9
  167.4 78.5 %copy-start.14 = (bf16[1024]{0:T(1024)(128)(2,1)S(1)}, bf16[1024]{0:T(1024)(128)(2,1)}, u32[]{:S(2)}) copy-start(bf16[1024]{0:T(1024)(128)(2,1)} %param.32) | copy-start | bytes 6148
  167.4 177.3 %copy-start.3 = (bf16[1024,352]{0,1:T(8,128)(2,1)S(1)}, bf16[1024,352]{0,1:T(8,128)(2,1)}, u32[]{:S(2)}) copy-start(bf16[1024,352]{0,1:T(8,128)(2,1)} %param.38) | copy-start | bytes 2162692
  168.4 213.9 %all-to-all-start = ((bf16[8,16,128]{2,1,0:T(8,128)(2,1)}), bf16[8,16,128]{2,1,0:T(8,128)(2,1)S(1)}, u32[]{:S(2)}, u32[]{:S(2)}) async-start(bf16[8,16,128]{2,1,0:T(8,128)(2,1)} %bitcast.35), calls=%async_computation | async-start | bytes 65536 | tf_op jit(solution)/shard_map/all_to_all | solution.py:162
  173.2 278.3 %all-reduce.5.cloned.1.call-start = ((), (), s32[]{:S(2)}) async-start(), calls=%async_computation.3 | async-start | bytes 524288 | tf_op jit(solution)/shard_map/psum | solution.py:159
  173.3 171.8 %copy-start.4 = (bf16[1024,352]{0,1:T(8,128)(2,1)S(1)}, bf16[1024,352]{0,1:T(8,128)(2,1)}, u32[]{:S(2)}) copy-start(bf16[1024,352]{0,1:T(8,128)(2,1)} %param.39) | copy-start | bytes 2162692
  245.8 131.4 %copy-start.15 = (bf16[1024]{0:T(1024)(128)(2,1)S(1)}, bf16[1024]{0:T(1024)(128)(2,1)}, u32[]{:S(2)}) copy-start(bf16[1024]{0:T(1024)(128)(2,1)} %param.33) | copy-start | bytes 6148
  245.8 131.4 %copy-start.8 = (bf16[1024,251]{1,0:T(8,128)(2,1)S(1)}, bf16[1024,251]{1,0:T(8,128)(2,1)}, u32[]{:S(2)}) copy-start(bf16[1024,251]{1,0:T(8,128)(2,1)} %param.41) | copy-start | bytes 1542148
  378.1 2.6 copy-start.2
  382.3 9.5 %all-to-all-start.1 = ((bf16[8,16,128]{2,1,0:T(8,128)(2,1)}), bf16[8,16,128]{2,1,0:T(8,128)(2,1)S(1)}, u32[]{:S(2)}, u32[]{:S(2)}) async-start(bf16[8,16,128]{2,1,0:T(8,128)(2,1)} %bitcast.37), calls=%async_computation.1 | async-start | bytes 65536 | tf_op jit(solution)/shard_map/all_to_all | solution.py:163
Sparse Core Ops, SparseCore 0:
  168.5 73.0 all-reduce.2
  382.4 68.9 all-reduce.4
